TPU v7x, 32 devices: a whole 2x2x4 slice. The times are simulated.
32 devices in a mesh: rows: 2 (over x), cols: 16 (over z, y, core).
Axes of the slice: x: 2, y: 2, z: 4, core: 2. Of those that a mesh axis runs over, the one named last changes fastest.
Arguments:
- queries: bfloat16 [8192, 1024], P(('rows', 'cols')), may hold values from -1 to 1
- attn_out: bfloat16 [8192, 1024], P(('rows', 'cols')), may hold values from -6 to 6
- out_grad: bfloat16 [8192, 1024], P(('rows', 'cols')), may hold values from -96 to 96
- log_norm: float32 [8192, 8], P(('rows', 'cols')), may hold values from 7.5 to 8.5
- leaf_kv: bfloat16 [8192, 256], P(('rows', 'cols')), may hold values from -1 to 1
- root_kv: bfloat16 [2048, 256], P('cols'), may hold values from -1 to 1
- branch_kv: bfloat16 [4, 1024, 256], P('rows', 'cols'), may hold values from -1 to 1
- branch_len: int32 [4], replicated, may hold values from 256 to 1024, as said below
- segment_ids: int32 [32, 256], P(('rows', 'cols')), may hold values from 0 to 7, never falling along the last dimension, each value on 1 to 128 neighbouring positions
- segment_branch: int32 [32, 8], P(('rows', 'cols')), may hold values from 0 to 1
Outputs:
- query_grad: bfloat16 [8192, 1024], P(('rows', 'cols'))
- leaf_kv_grad: float32 [8192, 256], P(('rows', 'cols'))
- root_kv_grad: float32 [2048, 256], P('cols')
- branch_kv_grad: float32 [4, 1024, 256], P('rows', 'cols')
Inputs may be any that keep to these rules, and one draw needn't show every extreme that they name: `branch_len`: every branch has between 256 and 1024 live slots; some branch has exactly 1024 and some exactly 256. `segment_ids`: never falling along a device's tokens; each segment has 1 to 128 tokens, one exactly 128. `segment_branch`: a segment on row r extends branch r * 2 + value.
All inputs are finite; a program needn't handle non-finite values.
Results may differ from a plain program's by a relative error of at most 0.0041.
Values may be sent and summed in bfloat16 or wider, within the bound.
A program may use at most 64 MiB of HBM per device.

v0:
```python
from functools import partial
import jax
import jax.numpy as jnp
from jax import lax
from jax.sharding import PartitionSpec as P

HEADS = 8
HD = 128
BR_DEV = 2
SEGS = 8


def block_grads(query_heads, grad_heads, log_norm, row_delta, key_rows, allowed):
    scale = HD ** (-0.5)
    keys_part = key_rows[:, :HD]
    values_part = key_rows[:, HD:]
    scores = (
        jnp.einsum("thd,kd->thk", query_heads, keys_part, preferred_element_type=jnp.float32)
        * scale
    )
    weights = jnp.where(allowed[:, None, :], jnp.exp(scores - log_norm[:, :, None]), 0.0)
    dweight = jnp.einsum("thd,kd->thk", grad_heads, values_part, preferred_element_type=jnp.float32)
    dscore = weights * (dweight - row_delta[:, :, None])
    weight_b = weights.astype(jnp.bfloat16)
    dscore_b = dscore.astype(jnp.bfloat16)
    query_part = (
        jnp.einsum("thk,kd->thd", dscore_b, keys_part, preferred_element_type=jnp.float32) * scale
    )
    key_grad = (
        jnp.einsum("thk,thd->kd", dscore_b, query_heads, preferred_element_type=jnp.float32) * scale
    )
    value_grad = jnp.einsum("thk,thd->kd", weight_b, grad_heads, preferred_element_type=jnp.float32)
    return (query_part, jnp.concatenate([key_grad, value_grad], axis=1))


def sweep_keys(query_heads, grad_heads, log_norm, row_delta, key_rows, allowed_of):
    count_rows = key_rows.shape[0]
    block_rows = 512 if count_rows % 512 == 0 else count_rows

    def visit_block(query_sum, block_index):
        offset = block_index * block_rows
        key_block = lax.dynamic_slice_in_dim(key_rows, offset, block_rows, 0)
        query_part, key_grads = block_grads(
            query_heads, grad_heads, log_norm, row_delta, key_block, allowed_of(offset, block_rows)
        )
        return (query_sum + query_part, key_grads)

    start_sum = jnp.zeros(query_heads.shape, jnp.float32)
    query_sum, key_grads = lax.scan(
        visit_block, start_sum, jnp.arange(count_rows // block_rows, dtype=jnp.int32)
    )
    return (query_sum, key_grads.reshape(count_rows, key_rows.shape[1]))


def shards(
    queries,
    attn_out,
    out_grad,
    log_norm,
    leaf_kv,
    root_kv,
    branch_kv,
    branch_len,
    segment_ids,
    segment_branch,
):
    tokens = queries.shape[0]
    query_heads = queries.reshape(tokens, HEADS, HD)
    grad_heads = out_grad.reshape(tokens, HEADS, HD)
    out_heads = attn_out.reshape(tokens, HEADS, HD)
    row_delta = jnp.sum(grad_heads.astype(jnp.float32) * out_heads.astype(jnp.float32), axis=2)
    segment = segment_ids[0]
    seg_branch = segment_branch[0]
    token_branch = jnp.sum(
        jnp.where(
            segment[:, None] == jnp.arange(SEGS, dtype=jnp.int32)[None, :], seg_branch[None, :], 0
        ),
        axis=1,
    )
    row_index = lax.axis_index("rows")
    lengths = lax.dynamic_slice_in_dim(branch_len, row_index * BR_DEV, BR_DEV, 0)
    run_keys = partial(sweep_keys, query_heads, grad_heads, log_norm, row_delta)

    def every_key(offset, count_rows):
        return jnp.ones((tokens, count_rows), dtype=bool)

    query_part, piece_grads = run_keys(
        lax.all_gather(root_kv, "cols", axis=0, tiled=True), every_key
    )
    root_grads = piece_grads
    query_grad = query_part
    piece = lax.all_gather(branch_kv, "cols", axis=1, tiled=True)
    branch_query_grad = query_grad
    updates = []
    for slot in range(BR_DEV):

        def slot_allowed(offset, count_rows, slot=slot):
            slot_pos = offset + jnp.arange(count_rows, dtype=jnp.int32)
            return (token_branch == slot)[:, None] & (slot_pos < lengths[slot])[None, :]

        query_part, piece_grads = run_keys(piece[slot], slot_allowed)
        branch_query_grad = branch_query_grad + query_part
        updates.append(piece_grads)
    branch_grads = jnp.stack(updates)
    query_grad = branch_query_grad
    positions = jnp.arange(tokens, dtype=jnp.int32)

    def leaf_allowed(offset, count_rows):
        key_pos = offset + jnp.arange(count_rows, dtype=jnp.int32)
        return (segment[:, None] == segment[None, :]) & (key_pos[None, :] <= positions[:, None])

    leaf_part, leaf_grads = run_keys(leaf_kv, leaf_allowed)
    query_grad = query_grad + leaf_part
    branch_grad = lax.psum_scatter(branch_grads, "cols", scatter_dimension=1, tiled=True)
    row_whole = lax.psum(root_grads, "rows")
    root_grad = lax.psum_scatter(row_whole, "cols", scatter_dimension=0, tiled=True)
    return (
        query_grad.reshape(tokens, HEADS * HD).astype(jnp.bfloat16),
        leaf_grads,
        root_grad,
        branch_grad,
    )


def solution(mesh):
    in_specs = (
        P(("rows", "cols"), None),
        P(("rows", "cols"), None),
        P(("rows", "cols"), None),
        P(("rows", "cols"), None),
        P(("rows", "cols"), None),
        P("cols", None),
        P("rows", "cols", None),
        P(),
        P(("rows", "cols"), None),
        P(("rows", "cols"), None),
    )
    out_specs = (
        P(("rows", "cols"), None),
        P(("rows", "cols"), None),
        P("cols", None),
        P("rows", "cols", None),
    )
    return jax.shard_map(shards, mesh=mesh, in_specs=in_specs, out_specs=out_specs, check_vma=False)
```

profile of v0, /device:TPU:0, one launch (start us, length us, event | category | flops | bytes accessed | tf_op | source)
XLA Modules:
  0.0 288.9 jit_solution(9851445871758798752)
XLA Ops:
  14.1 36.6 %all-gather.5.cloned.1.call-done = bf16[2,1024,256]{2,1,0:T(8,128)(2,1)} async-done(((bf16[2,64,256]{2,1,0:T(8,128)(2,1)}), bf16[2,1024,256]{2,1,0:T(8,128)(2,1)}) %all-gather.5.cloned.1.call-update) | async-done | bytes 1048592 | tf_op jit(solution)/shard_map/all_gather | solution.py:92
  50.8 2.2 slice_bitcast_fusion.1
  54.1 24.9 %while.46 = (s32[]{:T(128)}, f32[256,8,128]{2,0,1:T(8,128)}, f32[2,512,256]{2,1,0:T(8,128)}, s32[256]{0:T(256)S(1)}, s32[2]{0:T(128)S(1)}, /*index=5*/s32[2]{0:T...) while((s32[]{:T(128)}, f32[256,8,128]{2,0,1:T(8,128)}, ...), condition=%wide.region_7.8_spmd.clone, body=%wide.region_6.7_spmd.clone.sunk | while | flops 1353778432 | bytes 27552528 | solution.py:49
  56.8 1.6 fusion.157
  59.4 2.3 fusion.158
  62.5 2.7 fusion.159
  69.0 1.6 fusion.157
  71.6 2.3 fusion.158
  74.7 3.1 %fusion.159 = f32[256,8,128]{2,0,1:T(8,128)} fusion(bf16[256,8,512]{0,2,1:T(8,128)(2,1)S(1)} %fusion.158, f32[256,8,128]{2,0,1:T(8,128)} %get-tuple-element.584, pred[]{:T(512)S(6)} %compare.11, bf16[1024,256]{1,0:T(8,128)(2,1)} %get-tuple-element.605, s32[]{:T(128)S(6)} %select_n.70), kind=kOutput, calls=%fused_computation.54.clone.1 | convolution fusion | flops 269221888 | bytes 4325381 | tf_op jit(solution)/shard_map/while/body/eval_jaxpr/thk,kd->thd/dot_general | solution.py:27
  78.9 10.9 %all-gather.3.cloned.1.call-done = bf16[2048,256]{1,0:T(8,128)(2,1)} async-done(((bf16[128,256]{1,0:T(8,128)(2,1)}), bf16[2048,256]{1,0:T(8,128)(2,1)}) %all-gather.3.cloned.1.call-update) | async-done | bytes 1048592 | tf_op jit(solution)/shard_map/all_gather | solution.py:88
  89.9 42.4 %while.44 = (s32[]{:T(128)}, f32[256,8,128]{2,0,1:T(8,128)}, f32[4,512,256]{2,1,0:T(8,128)}, s32[4]{0:T(128)S(1)}, bf16[2048,256]{1,0:T(8,128)(2,1)}, /*index=5*...) while((s32[]{:T(128)}, f32[256,8,128]{2,0,1:T(8,128)}, ...), condition=%wide.region_2.3_spmd.clone, body=%wide.region_1.2_spmd.clone.sunk | while | flops 1351548928 | bytes 27156720 | solution.py:49
  91.1 1.6 fusion.134
  93.6 2.0 multiply_convert_fusion.3
  96.4 2.6 fusion.135
  101.4 1.6 fusion.134
  103.9 2.0 multiply_convert_fusion.3
  106.7 3.0 %fusion.135 = f32[256,8,128]{2,0,1:T(8,128)} fusion(bf16[512,256,8]{1,0,2:T(8,128)(2,1)S(1)} %multiply_convert_fusion.3, f32[256,8,128]{2,0,1:T(8,128)} %get-tuple-element.630, pred[]{:T(512)S(6)} %compare.9, bf16[2048,256]{1,0:T(8,128)(2,1)} %get-tuple-element.647, s32[]{:T(128)S(6)} %select_n.64), kind=kOutput, calls=%fused_computation.12.clone.1 | convolution fusion | flops 269221888 | bytes 4325381 | tf_op jit(solution)/shard_map/while/body/eval_jaxpr/thk,kd->thd/dot_general | solution.py:27
  112.1 1.6 fusion.134
  114.6 2.0 multiply_convert_fusion.3
  117.4 3.0 %fusion.135 = f32[256,8,128]{2,0,1:T(8,128)} fusion(bf16[512,256,8]{1,0,2:T(8,128)(2,1)S(1)} %multiply_convert_fusion.3, f32[256,8,128]{2,0,1:T(8,128)} %get-tuple-element.630, pred[]{:T(512)S(6)} %compare.9, bf16[2048,256]{1,0:T(8,128)(2,1)} %get-tuple-element.647, s32[]{:T(128)S(6)} %select_n.64), kind=kOutput, calls=%fused_computation.12.clone.1 | convolution fusion | flops 269221888 | bytes 4325381 | tf_op jit(solution)/shard_map/while/body/eval_jaxpr/thk,kd->thd/dot_general | solution.py:27
  122.8 1.6 fusion.134
  125.3 2.0 multiply_convert_fusion.3
  128.1 3.0 %fusion.135 = f32[256,8,128]{2,0,1:T(8,128)} fusion(bf16[512,256,8]{1,0,2:T(8,128)(2,1)S(1)} %multiply_convert_fusion.3, f32[256,8,128]{2,0,1:T(8,128)} %get-tuple-element.630, pred[]{:T(512)S(6)} %compare.9, bf16[2048,256]{1,0:T(8,128)(2,1)} %get-tuple-element.647, s32[]{:T(128)S(6)} %select_n.64), kind=kOutput, calls=%fused_computation.12.clone.1 | convolution fusion | flops 269221888 | bytes 4325381 | tf_op jit(solution)/shard_map/while/body/eval_jaxpr/thk,kd->thd/dot_general | solution.py:27
  133.6 17.1 %while.45 = (s32[]{:T(128)}, f32[256,8,128]{2,0,1:T(8,128)S(1)}, f32[2,512,256]{2,1,0:T(8,128)}, s32[256]{0:T(256)S(1)}, s32[2]{0:T(128)S(1)}, /*index=5*/s32[2]...) while((s32[]{:T(128)}, f32[256,8,128]{2,0,1:T(8,128)S(1)}, ...), condition=%wide.region_5.6_spmd.clone, body=%wide.region_4.5_spmd.clone.sunk | while | flops 1353778432 | bytes 29649700 | solution.py:49
  135.0 1.6 fusion.145
  143.5 1.6 fusion.145
  150.7 3.0 %pad_maximum_fusion = f32[2,1024,256]{2,1,0:T(8,128)} fusion(f32[1,1024,256]{2,1,0:T(8,128)} %bitcast.248, f32[1,1024,256]{2,1,0:T(8,128)} %bitcast.247), kind=kLoop, calls=%fused_computation.70 | loop fusion | flops 524288 | bytes 4194304 | tf_op jit(solution)/shard_map/stack | solution.py:104
  161.2 32.0 %reduce-scatter.5.cloned.1.call-done = f32[128,256]{1,0:T(8,128)} async-done(((f32[2048,256]{1,0:T(8,128)}), f32[128,256]{1,0:T(8,128)}) %reduce-scatter.5.cloned.1.call-update) | async-done | bytes 131088 | tf_op jit(solution)/shard_map/reduce_scatter | solution.py:116
  193.2 2.5 fusion.60
  195.8 2.0 copy.70
  197.8 60.3 %reduce-scatter.3.cloned.1.call-done = f32[2,64,256]{2,1,0:T(8,128)} async-done(((f32[2,1024,256]{2,1,0:T(8,128)}), f32[2,64,256]{2,1,0:T(8,128)}) %reduce-scatter.3.cloned.1.call-update) | async-done | bytes 131088 | tf_op jit(solution)/shard_map/reduce_scatter | solution.py:114
  258.1 22.6 %all-reduce.2.cloned.1.call-done = f32[128,256]{1,0:T(8,128)} async-done(((f32[128,256]{1,0:T(8,128)}), f32[128,256]{1,0:T(8,128)}) %all-reduce.2.cloned.1.call-update) | async-done | bytes 131088 | tf_op jit(solution)/shard_map/psum | solution.py:115
  (112 shorter events, 54.0 us)
Async XLA Ops:
  7.2 43.6 %all-gather.5.cloned.1.call-start = ((), (), s32[]{:S(2)}) async-start(), calls=%async_computation.3 | async-start | bytes 1114112 | tf_op jit(solution)/shard_map/all_gather | solution.py:92
  7.9 82.0 %all-gather.3.cloned.1.call-start = ((), (), s32[]{:S(2)}) async-start(), calls=%async_computation.2 | async-start | bytes 1114112 | tf_op jit(solution)/shard_map/all_gather | solution.py:88
  8.6 184.6 %reduce-scatter.5.cloned.1.call-start = ((), (), s32[]{:S(2)}) async-start(), calls=%async_computation.5 | async-start | bytes 2228224 | tf_op jit(solution)/shard_map/reduce_scatter | solution.py:116
  8.7 45.3 %copy-start.1 = (f32[256,8]{0,1:T(8,128)S(1)}, f32[256,8]{0,1:T(8,128)}, u32[]{:S(2)}) copy-start(f32[256,8]{0,1:T(8,128)} %param.19) | copy-start | bytes 24580
  132.3 125.9 %reduce-scatter.3.cloned.1.call-start = ((), (), s32[]{:S(2)}) async-start(), calls=%async_computation.4 | async-start | bytes 2228224 | tf_op jit(solution)/shard_map/reduce_scatter | solution.py:114
  136.6 1.1 copy-start
  145.1 1.1 copy-start
  150.7 3.1 %copy-start.3 = (s32[1,256]{1,0:T(1,128)S(1)}, s32[1,256]{1,0:T(1,128)}, u32[]{:S(2)}) copy-start(s32[1,256]{1,0:T(1,128)} %param.24) | copy-start | bytes 3076
  150.7 3.2 %copy-start.2 = (bf16[256,256]{1,0:T(8,128)(2,1)S(1)}, bf16[256,256]{1,0:T(8,128)(2,1)}, u32[]{:S(2)}) copy-start(bf16[256,256]{1,0:T(8,128)(2,1)} %param.20) | copy-start | bytes 393220
  153.7 127.0 %all-reduce.2.cloned.1.call-start = ((), (), s32[]{:S(2)}) async-start(), calls=%async_computation.6 | async-start | bytes 262144 | tf_op jit(solution)/shard_map/psum | solution.py:115
Sparse Core Ops, SparseCore 0:
  10.2 40.5 all-gather.4
  52.9 36.8 all-gather.2
  132.4 60.7 reduce-scatter.4
  197.4 60.7 reduce-scatter.2
  260.3 20.4 all-reduce.1
where the time goes:
time: 290 us; the launch traced here: 289 us
  waiting for transfers between devices  164 us (57%)
  matrix products  66.6 us (23%)
  local copies, waits for them, and re-layouts  32.1 us (11%)
  between operations  13.9 us (5%)
  other arithmetic  6.25 us (2%)
  loops' own time  5.64 us (2%)
    reduce_scatter x1, waiting for transfers between devices, shards(): lax.psum_scatter(branch_grads, 'cols', scatter_dimension=1, tiled=True)  60.3 us
    all_gather x1, waiting for transfers between devices, shards(): piece = lax.all_gather(branch_kv, 'cols', axis=1, tiled=True)  36.6 us
    reduce_scatter x1, waiting for transfers between devices, shards(): lax.psum_scatter(row_whole, 'cols', scatter_dimension=0, tiled=True)  32 us
    psum x1, waiting for transfers between devices, shards(): row_whole = lax.psum(root_grads, 'rows')  22.6 us
    dot_general x9, matrix products, block_grads(): jnp.einsum('thk,kd->thd', dscore_b, keys_part, preferred_element_type=jnp...  22.4 us
    dot_general x9, matrix products, block_grads(): jnp.einsum('thd,kd->thk', grad_heads, values_part, preferred_element_type...  15.8 us
    dot_general x9, matrix products, block_grads(): jnp.einsum('thd,kd->thk', query_heads, keys_part, preferred_element_type=...  13.5 us
    all_gather x1, waiting for transfers between devices, shards(): lax.all_gather(root_kv, 'cols', axis=0, tiled=True)  10.9 us
  transfers between devices with their start and end apart: 5, of which 5 were waited for; matrix products, arithmetic and copies ran while one was open for 22% of the time, Pallas kernels for 0%

commit v1 on v0

--- a/solution.py
+++ b/solution.py
@@ -8,6 +8,22 @@
 HD = 128
 BR_DEV = 2
 SEGS = 8
+
+
+def collect(x, axis, dim):
+    ways, here, step = (lax.axis_size(axis), lax.axis_index(axis), x.shape[dim])
+    shape = [n * ways if d == dim else n for d, n in enumerate(x.shape)]
+    full = lax.dynamic_update_slice_in_dim(jnp.zeros(shape, x.dtype), x, here * step, axis=dim)
+    going_up = going_down = x
+    for far in range(1, ways // 2 + 1):
+        going_up = lax.ppermute(going_up, axis, [(d, (d + 1) % ways) for d in range(ways)])
+        full = lax.dynamic_update_slice_in_dim(full, going_up, (here - far) % ways * step, axis=dim)
+        if 2 * far < ways:
+            going_down = lax.ppermute(going_down, axis, [(d, (d - 1) % ways) for d in range(ways)])
+            full = lax.dynamic_update_slice_in_dim(
+                full, going_down, (here + far) % ways * step, axis=dim
+            )
+    return full
 
 
 def block_grads(query_heads, grad_heads, log_norm, row_delta, key_rows, allowed):
@@ -89,7 +105,7 @@
     )
     root_grads = piece_grads
     query_grad = query_part
-    piece = lax.all_gather(branch_kv, "cols", axis=1, tiled=True)
+    piece = collect(branch_kv, "cols", 1)
     branch_query_grad = query_grad
     updates = []
     for slot in range(BR_DEV):

time: 290 us -> 294 us (1.014)
  starting transfers between devices: 0.38 us -> 33.2 us
  waiting for transfers between devices: 164 us -> 137 us
    all_gather x1 -> x0, waiting for transfers between devices: 36.6 us -> none  [shards(): piece = lax.all_gather(branch_kv, 'cols', axis=1, tiled=True)]
    ppermute x0 -> x15, starting transfers between devices: none -> 32.9 us  [the longest x7 32.9 us: collect(): lax.ppermute(going_down, axis, [(d, (d - 1) % ways) for d in range(ways)])]
    ppermute x0 -> x15, waiting for transfers between devices: none -> 23.2 us  [the longest x8 16.2 us: collect(): lax.ppermute(going_up, axis, [(d, (d + 1) % ways) for d in range(ways)])]
    all_gather x1, waiting for transfers between devices: 10.9 us -> 0.01 us  [shards(): lax.all_gather(root_kv, 'cols', axis=0, tiled=True)]
    unnamed x11 -> x17, local copies, waits for them, and re-layouts: 6.95 us -> 6.96 us
  transfers between devices with their start and end apart: 5 -> 19, of which waited for: 5 -> 15; matrix products, arithmetic and copies ran while one was open for 22% -> 21% of each run, Pallas kernels for 0% -> 0%
where the time goes in v1:
time: 294 us; the launch traced here: 293 us
  waiting for transfers between devices  137 us (47%)
  matrix products  66.6 us (23%)
  starting transfers between devices  33.2 us (11%)
  local copies, waits for them, and re-layouts  30.5 us (10%)
  between operations  14.5 us (5%)
  loops' own time  5.65 us (2%)
  other arithmetic  5.54 us (2%)
    reduce_scatter x1, waiting for transfers between devices, shards(): lax.psum_scatter(branch_grads, 'cols', scatter_dimension=1, tiled=True)  60.5 us
    ppermute x7, starting transfers between devices, collect(): lax.ppermute(going_down, axis, [(d, (d - 1) % ways) for d in range(ways)])  32.9 us
    reduce_scatter x1, waiting for transfers between devices, shards(): lax.psum_scatter(row_whole, 'cols', scatter_dimension=0, tiled=True)  30.2 us
    psum x1, waiting for transfers between devices, shards(): row_whole = lax.psum(root_grads, 'rows')  22.6 us
    dot_general x9, matrix products, block_grads(): jnp.einsum('thk,kd->thd', dscore_b, keys_part, preferred_element_type=jnp...  22.3 us
    ppermute x8, waiting for transfers between devices, collect(): lax.ppermute(going_up, axis, [(d, (d + 1) % ways) for d in range(ways)])  16.2 us
    dot_general x9, matrix products, block_grads(): jnp.einsum('thd,kd->thk', grad_heads, values_part, preferred_element_type...  15.8 us
    dot_general x9, matrix products, block_grads(): jnp.einsum('thd,kd->thk', query_heads, keys_part, preferred_element_type=...  13.5 us
  transfers between devices with their start and end apart: 19, of which 15 were waited for; matrix products, arithmetic and copies ran while one was open for 21% of the time, Pallas kernels for 0%

profile of v1, /device:TPU:0, one launch (start us, length us, event | category | flops | bytes accessed | tf_op | source)
XLA Modules:
  0.0 292.5 jit_solution(3403272012570976592)
XLA Ops:
  7.3 5.5 %collective-permute-start.1 = (bf16[2,64,256]{2,1,0:T(8,128)(2,1)}, bf16[2,64,256]{2,1,0:T(8,128)(2,1)S(1)}, u32[]{:S(2)}, u32[]{:S(2)}) collective-permute-start(bf16[2,64,256]{2,1,0:T(8,128)(2,1)} %param.22), channel_id=1, source_target_pairs={{0,15},{1,0},{2,1},{3,2},{4,3},{5,4},{6,5},{7,6},{8,7},{9,8},{10,9... | collective-permute-start | bytes 196616 | tf_op jit(solution)/shard_map/ppermute | solution.py:22
  17.5 4.5 %collective-permute-start.3 = (bf16[2,64,256]{2,1,0:T(8,128)(2,1)S(1)}, bf16[2,64,256]{2,1,0:T(8,128)(2,1)S(1)}, u32[]{:S(2)}, u32[]{:S(2)}) collective-permute-start(bf16[2,64,256]{2,1,0:T(8,128)(2,1)S(1)} %collective-permute-done.1), channel_id=1, source_target_pairs={{0,15},{1,0},{2,1},{3,2},{4,3},{5,4},{6,5},{7,6},{8,7},{9,8},{10,9... | collective-permute-start | bytes 196616 | tf_op jit(solution)/shard_map/ppermute | solution.py:22
  22.0 2.1 collective-permute-done.3
  24.0 4.6 %collective-permute-start.5 = (bf16[2,64,256]{2,1,0:T(8,128)(2,1)S(1)}, bf16[2,64,256]{2,1,0:T(8,128)(2,1)S(1)}, u32[]{:S(2)}, u32[]{:S(2)}) collective-permute-start(bf16[2,64,256]{2,1,0:T(8,128)(2,1)S(1)} %collective-permute-done.3), channel_id=1, source_target_pairs={{0,15},{1,0},{2,1},{3,2},{4,3},{5,4},{6,5},{7,6},{8,7},{9,8},{10,9... | collective-permute-start | bytes 196616 | tf_op jit(solution)/shard_map/ppermute | solution.py:22
  30.5 4.6 %collective-permute-start.7 = (bf16[2,64,256]{2,1,0:T(8,128)(2,1)S(1)}, bf16[2,64,256]{2,1,0:T(8,128)(2,1)S(1)}, u32[]{:S(2)}, u32[]{:S(2)}) collective-permute-start(bf16[2,64,256]{2,1,0:T(8,128)(2,1)S(1)} %collective-permute-done.5), channel_id=1, source_target_pairs={{0,15},{1,0},{2,1},{3,2},{4,3},{5,4},{6,5},{7,6},{8,7},{9,8},{10,9... | collective-permute-start | bytes 196616 | tf_op jit(solution)/shard_map/ppermute | solution.py:22
  37.1 4.5 %collective-permute-start.9 = (bf16[2,64,256]{2,1,0:T(8,128)(2,1)S(1)}, bf16[2,64,256]{2,1,0:T(8,128)(2,1)S(1)}, u32[]{:S(2)}, u32[]{:S(2)}) collective-permute-start(bf16[2,64,256]{2,1,0:T(8,128)(2,1)S(1)} %collective-permute-done.7), channel_id=1, source_target_pairs={{0,15},{1,0},{2,1},{3,2},{4,3},{5,4},{6,5},{7,6},{8,7},{9,8},{10,9... | collective-permute-start | bytes 196616 | tf_op jit(solution)/shard_map/ppermute | solution.py:22
  43.5 4.6 %collective-permute-start.11 = (bf16[2,64,256]{2,1,0:T(8,128)(2,1)S(1)}, bf16[2,64,256]{2,1,0:T(8,128)(2,1)S(1)}, u32[]{:S(2)}, u32[]{:S(2)}) collective-permute-start(bf16[2,64,256]{2,1,0:T(8,128)(2,1)S(1)} %collective-permute-done.9), channel_id=1, source_target_pairs={{0,15},{1,0},{2,1},{3,2},{4,3},{5,4},{6,5},{7,6},{8,7},{9,8},{10,9... | collective-permute-start | bytes 196616 | tf_op jit(solution)/shard_map/ppermute | solution.py:22
  50.0 4.6 %collective-permute-start.13 = (bf16[2,64,256]{2,1,0:T(8,128)(2,1)S(1)}, bf16[2,64,256]{2,1,0:T(8,128)(2,1)S(1)}, u32[]{:S(2)}, u32[]{:S(2)}) collective-permute-start(bf16[2,64,256]{2,1,0:T(8,128)(2,1)S(1)} %collective-permute-done.11), channel_id=1, source_target_pairs={{0,15},{1,0},{2,1},{3,2},{4,3},{5,4},{6,5},{7,6},{8,7},{9,8},{10,9... | collective-permute-start | bytes 196616 | tf_op jit(solution)/shard_map/ppermute | solution.py:22
  55.5 6.4 %collective-permute-done.12 = bf16[2,64,256]{2,1,0:T(8,128)(2,1)S(1)} collective-permute-done((bf16[2,64,256]{2,1,0:T(8,128)(2,1)S(1)}, bf16[2,64,256]{2,1,0:T(8,128)(2,1)S(1)}, u32[]{:S(2)}, u32[]{:S(2)}) %collective-permute-start.12) | collective-permute-done | bytes 65568 | tf_op jit(solution)/shard_map/ppermute | solution.py:19
  61.9 6.3 %collective-permute-done.14 = bf16[2,64,256]{2,1,0:T(8,128)(2,1)S(1)} collective-permute-done((bf16[2,64,256]{2,1,0:T(8,128)(2,1)S(1)}, bf16[2,64,256]{2,1,0:T(8,128)(2,1)S(1)}, u32[]{:S(2)}, u32[]{:S(2)}) %collective-permute-start.14) | collective-permute-done | bytes 65568 | tf_op jit(solution)/shard_map/ppermute | solution.py:19
  70.3 24.8 %while.46 = (s32[]{:T(128)}, f32[256,8,128]{2,0,1:T(8,128)}, f32[2,512,256]{2,1,0:T(8,128)}, s32[256]{0:T(256)S(1)}, s32[2]{0:T(128)S(1)}, /*index=5*/s32[2]{0:T...) while((s32[]{:T(128)}, f32[256,8,128]{2,0,1:T(8,128)}, ...), condition=%wide.region_7.8_spmd.clone, body=%wide.region_6.7_spmd.clone.sunk | while | flops 1353778432 | bytes 27552528 | solution.py:65
  75.7 2.3 fusion.158
  78.8 2.7 fusion.159
  87.9 2.3 fusion.158
  91.0 3.1 %fusion.159 = f32[256,8,128]{2,0,1:T(8,128)} fusion(bf16[256,8,512]{0,2,1:T(8,128)(2,1)S(1)} %fusion.158, f32[256,8,128]{2,0,1:T(8,128)} %get-tuple-element.584, pred[]{:T(512)S(6)} %compare.26, bf16[1024,256]{1,0:T(8,128)(2,1)} %get-tuple-element.605, s32[]{:T(128)S(6)} %select_n.212), kind=kOutput, calls=%fused_computation.54.clone.1 | convolution fusion | flops 269221888 | bytes 4325381 | tf_op jit(solution)/shard_map/while/body/eval_jaxpr/thk,kd->thd/dot_general | solution.py:43
  95.1 42.5 %while.44 = (s32[]{:T(128)}, f32[256,8,128]{2,0,1:T(8,128)}, f32[4,512,256]{2,1,0:T(8,128)}, s32[4]{0:T(128)S(1)}, bf16[2048,256]{1,0:T(8,128)(2,1)}, /*index=5*...) while((s32[]{:T(128)}, f32[256,8,128]{2,0,1:T(8,128)}, ...), condition=%wide.region_2.3_spmd.clone, body=%wide.region_1.2_spmd.clone.sunk | while | flops 1351548928 | bytes 27156720 | solution.py:65
  98.9 2.0 multiply_convert_fusion.3
  101.7 2.7 fusion.135
  109.2 2.0 multiply_convert_fusion.3
  112.0 3.1 %fusion.135 = f32[256,8,128]{2,0,1:T(8,128)} fusion(bf16[512,256,8]{1,0,2:T(8,128)(2,1)S(1)} %multiply_convert_fusion.3, f32[256,8,128]{2,0,1:T(8,128)} %get-tuple-element.630, pred[]{:T(512)S(6)} %compare.24, bf16[2048,256]{1,0:T(8,128)(2,1)} %get-tuple-element.647, s32[]{:T(128)S(6)} %select_n.206), kind=kOutput, calls=%fused_computation.12.clone.1 | convolution fusion | flops 269221888 | bytes 4325381 | tf_op jit(solution)/shard_map/while/body/eval_jaxpr/thk,kd->thd/dot_general | solution.py:43
  117.4 1.6 fusion.134
  119.9 2.0 multiply_convert_fusion.3
  122.7 3.1 %fusion.135 = f32[256,8,128]{2,0,1:T(8,128)} fusion(bf16[512,256,8]{1,0,2:T(8,128)(2,1)S(1)} %multiply_convert_fusion.3, f32[256,8,128]{2,0,1:T(8,128)} %get-tuple-element.630, pred[]{:T(512)S(6)} %compare.24, bf16[2048,256]{1,0:T(8,128)(2,1)} %get-tuple-element.647, s32[]{:T(128)S(6)} %select_n.206), kind=kOutput, calls=%fused_computation.12.clone.1 | convolution fusion | flops 269221888 | bytes 4325381 | tf_op jit(solution)/shard_map/while/body/eval_jaxpr/thk,kd->thd/dot_general | solution.py:43
  130.6 2.0 multiply_convert_fusion.3
  133.4 3.1 %fusion.135 = f32[256,8,128]{2,0,1:T(8,128)} fusion(bf16[512,256,8]{1,0,2:T(8,128)(2,1)S(1)} %multiply_convert_fusion.3, f32[256,8,128]{2,0,1:T(8,128)} %get-tuple-element.630, pred[]{:T(512)S(6)} %compare.24, bf16[2048,256]{1,0:T(8,128)(2,1)} %get-tuple-element.647, s32[]{:T(128)S(6)} %select_n.206), kind=kOutput, calls=%fused_computation.12.clone.1 | convolution fusion | flops 269221888 | bytes 4325381 | tf_op jit(solution)/shard_map/while/body/eval_jaxpr/thk,kd->thd/dot_general | solution.py:43
  139.0 17.1 %while.45 = (s32[]{:T(128)}, f32[256,8,128]{2,0,1:T(8,128)S(1)}, f32[2,512,256]{2,1,0:T(8,128)}, s32[256]{0:T(256)S(1)}, s32[2]{0:T(128)S(1)}, /*index=5*/s32[2]...) while((s32[]{:T(128)}, f32[256,8,128]{2,0,1:T(8,128)S(1)}, ...), condition=%wide.region_5.6_spmd.clone, body=%wide.region_4.5_spmd.clone.sunk | while | flops 1353778432 | bytes 29649700 | solution.py:65
  156.1 3.0 %pad_maximum_fusion = f32[2,1024,256]{2,1,0:T(8,128)} fusion(f32[1,1024,256]{2,1,0:T(8,128)} %bitcast.248, f32[1,1024,256]{2,1,0:T(8,128)} %bitcast.247), kind=kLoop, calls=%fused_computation.70 | loop fusion | flops 524288 | bytes 4194304 | tf_op jit(solution)/shard_map/stack | solution.py:120
  166.5 30.2 %reduce-scatter.5.cloned.1.call-done = f32[128,256]{1,0:T(8,128)} async-done(((f32[2048,256]{1,0:T(8,128)}), f32[128,256]{1,0:T(8,128)}) %reduce-scatter.5.cloned.1.call-update) | async-done | bytes 131088 | tf_op jit(solution)/shard_map/reduce_scatter | solution.py:132
  196.7 2.5 fusion.60
  199.3 2.0 copy.70
  201.3 60.5 %reduce-scatter.3.cloned.1.call-done = f32[2,64,256]{2,1,0:T(8,128)} async-done(((f32[2,1024,256]{2,1,0:T(8,128)}), f32[2,64,256]{2,1,0:T(8,128)}) %reduce-scatter.3.cloned.1.call-update) | async-done | bytes 131088 | tf_op jit(solution)/shard_map/reduce_scatter | solution.py:130
  261.8 22.6 %all-reduce.2.cloned.1.call-done = f32[128,256]{1,0:T(8,128)} async-done(((f32[128,256]{1,0:T(8,128)}), f32[128,256]{1,0:T(8,128)}) %all-reduce.2.cloned.1.call-update) | async-done | bytes 131088 | tf_op jit(solution)/shard_map/psum | solution.py:131
  (162 shorter events, 72.2 us)
Async XLA Ops:
  7.2 10.1 %copy-start.3 = (bf16[2,64,256]{2,1,0:T(8,128)(2,1)S(1)}, bf16[2,64,256]{2,1,0:T(8,128)(2,1)}, u32[]{:S(2)}) copy-start(bf16[2,64,256]{2,1,0:T(8,128)(2,1)} %param.22) | copy-start | bytes 196612
  7.2 9.8 %copy-start.6 = (s32[4]{0:T(128)S(1)}, s32[4]{0:T(128)}, u32[]{:S(2)}) copy-start(s32[4]{0:T(128)} %param.23) | copy-start | bytes 52
  7.2 10.2 %copy-start.5 = (s32[1,8]{1,0:T(1,128)S(1)}, s32[1,8]{1,0:T(1,128)}, u32[]{:S(2)}) copy-start(s32[1,8]{1,0:T(1,128)} %param.25) | copy-start | bytes 100
  7.2 10.2 %copy-start.4 = (s32[1,256]{1,0:T(1,128)S(1)}, s32[1,256]{1,0:T(1,128)}, u32[]{:S(2)}) copy-start(s32[1,256]{1,0:T(1,128)} %param.24) | copy-start | bytes 3076
  7.2 87.9 %all-gather.2.cloned.1.call-start = ((), (), s32[]{:S(2)}) async-start(), calls=%async_computation.2 | async-start | bytes 1114112 | tf_op jit(solution)/shard_map/all_gather | solution.py:104
  7.3 10.2 %collective-permute-start.1 = (bf16[2,64,256]{2,1,0:T(8,128)(2,1)}, bf16[2,64,256]{2,1,0:T(8,128)(2,1)S(1)}, u32[]{:S(2)}, u32[]{:S(2)}) collective-permute-start(bf16[2,64,256]{2,1,0:T(8,128)(2,1)} %param.22), channel_id=1, source_target_pairs={{0,15},{1,0},{2,1},{3,2},{4,3},{5,4},{6,5},{7,6},{8,7},{9,8},{10,9... | collective-permute-start | bytes 196616 | tf_op jit(solution)/shard_map/ppermute | solution.py:22
  12.8 9.2 %collective-permute-start = (bf16[2,64,256]{2,1,0:T(8,128)(2,1)}, bf16[2,64,256]{2,1,0:T(8,128)(2,1)S(1)}, u32[]{:S(2)}, u32[]{:S(2)}) collective-permute-start(bf16[2,64,256]{2,1,0:T(8,128)(2,1)} %param.22), channel_id=1, source_target_pairs={{0,1},{1,2},{2,3},{3,4},{4,5},{5,6},{6,7},{7,8},{8,9},{9,10},{10,1... | collective-permute-start | bytes 196616 | tf_op jit(solution)/shard_map/ppermute | solution.py:19
  12.8 183.9 %reduce-scatter.5.cloned.1.call-start = ((), (), s32[]{:S(2)}) async-start(), calls=%async_computation.4 | async-start | bytes 2228224 | tf_op jit(solution)/shard_map/reduce_scatter | solution.py:132
  16.9 53.4 %copy-start.1 = (f32[256,8]{0,1:T(8,128)S(1)}, f32[256,8]{0,1:T(8,128)}, u32[]{:S(2)}) copy-start(f32[256,8]{0,1:T(8,128)} %param.19) | copy-start | bytes 24580
  17.5 6.6 %collective-permute-start.3 = (bf16[2,64,256]{2,1,0:T(8,128)(2,1)S(1)}, bf16[2,64,256]{2,1,0:T(8,128)(2,1)S(1)}, u32[]{:S(2)}, u32[]{:S(2)}) collective-permute-start(bf16[2,64,256]{2,1,0:T(8,128)(2,1)S(1)} %collective-permute-done.1), channel_id=1, source_target_pairs={{0,15},{1,0},{2,1},{3,2},{4,3},{5,4},{6,5},{7,6},{8,7},{9,8},{10,9... | collective-permute-start | bytes 196616 | tf_op jit(solution)/shard_map/ppermute | solution.py:22
  21.9 7.0 %collective-permute-start.2 = (bf16[2,64,256]{2,1,0:T(8,128)(2,1)S(1)}, bf16[2,64,256]{2,1,0:T(8,128)(2,1)S(1)}, u32[]{:S(2)}, u32[]{:S(2)}) collective-permute-start(bf16[2,64,256]{2,1,0:T(8,128)(2,1)S(1)} %collective-permute-done), channel_id=1, source_target_pairs={{0,1},{1,2},{2,3},{3,4},{4,5},{5,6},{6,7},{7,8},{8,9},{9,10},{10,1... | collective-permute-start | bytes 196616 | tf_op jit(solution)/shard_map/ppermute | solution.py:19
  24.0 6.5 %collective-permute-start.5 = (bf16[2,64,256]{2,1,0:T(8,128)(2,1)S(1)}, bf16[2,64,256]{2,1,0:T(8,128)(2,1)S(1)}, u32[]{:S(2)}, u32[]{:S(2)}) collective-permute-start(bf16[2,64,256]{2,1,0:T(8,128)(2,1)S(1)} %collective-permute-done.3), channel_id=1, source_target_pairs={{0,15},{1,0},{2,1},{3,2},{4,3},{5,4},{6,5},{7,6},{8,7},{9,8},{10,9... | collective-permute-start | bytes 196616 | tf_op jit(solution)/shard_map/ppermute | solution.py:22
  29.0 6.8 %collective-permute-start.4 = (bf16[2,64,256]{2,1,0:T(8,128)(2,1)S(1)}, bf16[2,64,256]{2,1,0:T(8,128)(2,1)S(1)}, u32[]{:S(2)}, u32[]{:S(2)}) collective-permute-start(bf16[2,64,256]{2,1,0:T(8,128)(2,1)S(1)} %collective-permute-done.2), channel_id=1, source_target_pairs={{0,1},{1,2},{2,3},{3,4},{4,5},{5,6},{6,7},{7,8},{8,9},{9,10},{10,1... | collective-permute-start | bytes 196616 | tf_op jit(solution)/shard_map/ppermute | solution.py:19
  30.5 6.5 %collective-permute-start.7 = (bf16[2,64,256]{2,1,0:T(8,128)(2,1)S(1)}, bf16[2,64,256]{2,1,0:T(8,128)(2,1)S(1)}, u32[]{:S(2)}, u32[]{:S(2)}) collective-permute-start(bf16[2,64,256]{2,1,0:T(8,128)(2,1)S(1)} %collective-permute-done.5), channel_id=1, source_target_pairs={{0,15},{1,0},{2,1},{3,2},{4,3},{5,4},{6,5},{7,6},{8,7},{9,8},{10,9... | collective-permute-start | bytes 196616 | tf_op jit(solution)/shard_map/ppermute | solution.py:22
  35.7 6.5 %collective-permute-start.6 = (bf16[2,64,256]{2,1,0:T(8,128)(2,1)S(1)}, bf16[2,64,256]{2,1,0:T(8,128)(2,1)S(1)}, u32[]{:S(2)}, u32[]{:S(2)}) collective-permute-start(bf16[2,64,256]{2,1,0:T(8,128)(2,1)S(1)} %collective-permute-done.4), channel_id=1, source_target_pairs={{0,1},{1,2},{2,3},{3,4},{4,5},{5,6},{6,7},{7,8},{8,9},{9,10},{10,1... | collective-permute-start | bytes 196616 | tf_op jit(solution)/shard_map/ppermute | solution.py:19
  37.1 6.4 %collective-permute-start.9 = (bf16[2,64,256]{2,1,0:T(8,128)(2,1)S(1)}, bf16[2,64,256]{2,1,0:T(8,128)(2,1)S(1)}, u32[]{:S(2)}, u32[]{:S(2)}) collective-permute-start(bf16[2,64,256]{2,1,0:T(8,128)(2,1)S(1)} %collective-permute-done.7), channel_id=1, source_target_pairs={{0,15},{1,0},{2,1},{3,2},{4,3},{5,4},{6,5},{7,6},{8,7},{9,8},{10,9... | collective-permute-start | bytes 196616 | tf_op jit(solution)/shard_map/ppermute | solution.py:22
  42.2 6.9 %collective-permute-start.8 = (bf16[2,64,256]{2,1,0:T(8,128)(2,1)S(1)}, bf16[2,64,256]{2,1,0:T(8,128)(2,1)S(1)}, u32[]{:S(2)}, u32[]{:S(2)}) collective-permute-start(bf16[2,64,256]{2,1,0:T(8,128)(2,1)S(1)} %collective-permute-done.6), channel_id=1, source_target_pairs={{0,1},{1,2},{2,3},{3,4},{4,5},{5,6},{6,7},{7,8},{8,9},{9,10},{10,1... | collective-permute-start | bytes 196616 | tf_op jit(solution)/shard_map/ppermute | solution.py:19
  43.5 6.5 %collective-permute-start.11 = (bf16[2,64,256]{2,1,0:T(8,128)(2,1)S(1)}, bf16[2,64,256]{2,1,0:T(8,128)(2,1)S(1)}, u32[]{:S(2)}, u32[]{:S(2)}) collective-permute-start(bf16[2,64,256]{2,1,0:T(8,128)(2,1)S(1)} %collective-permute-done.9), channel_id=1, source_target_pairs={{0,15},{1,0},{2,1},{3,2},{4,3},{5,4},{6,5},{7,6},{8,7},{9,8},{10,9... | collective-permute-start | bytes 196616 | tf_op jit(solution)/shard_map/ppermute | solution.py:22
  49.1 6.4 %collective-permute-start.10 = (bf16[2,64,256]{2,1,0:T(8,128)(2,1)S(1)}, bf16[2,64,256]{2,1,0:T(8,128)(2,1)S(1)}, u32[]{:S(2)}, u32[]{:S(2)}) collective-permute-start(bf16[2,64,256]{2,1,0:T(8,128)(2,1)S(1)} %collective-permute-done.8), channel_id=1, source_target_pairs={{0,1},{1,2},{2,3},{3,4},{4,5},{5,6},{6,7},{7,8},{8,9},{9,10},{10,1... | collective-permute-start | bytes 196616 | tf_op jit(solution)/shard_map/ppermute | solution.py:19
  50.0 11.9 %collective-permute-start.13 = (bf16[2,64,256]{2,1,0:T(8,128)(2,1)S(1)}, bf16[2,64,256]{2,1,0:T(8,128)(2,1)S(1)}, u32[]{:S(2)}, u32[]{:S(2)}) collective-permute-start(bf16[2,64,256]{2,1,0:T(8,128)(2,1)S(1)} %collective-permute-done.11), channel_id=1, source_target_pairs={{0,15},{1,0},{2,1},{3,2},{4,3},{5,4},{6,5},{7,6},{8,7},{9,8},{10,9... | collective-permute-start | bytes 196616 | tf_op jit(solution)/shard_map/ppermute | solution.py:22
  55.5 6.4 %collective-permute-start.12 = (bf16[2,64,256]{2,1,0:T(8,128)(2,1)S(1)}, bf16[2,64,256]{2,1,0:T(8,128)(2,1)S(1)}, u32[]{:S(2)}, u32[]{:S(2)}) collective-permute-start(bf16[2,64,256]{2,1,0:T(8,128)(2,1)S(1)} %collective-permute-done.10), channel_id=1, source_target_pairs={{0,1},{1,2},{2,3},{3,4},{4,5},{5,6},{6,7},{7,8},{8,9},{9,10},{10,1... | collective-permute-start | bytes 196616 | tf_op jit(solution)/shard_map/ppermute | solution.py:19
  61.9 6.4 %collective-permute-start.14 = (bf16[2,64,256]{2,1,0:T(8,128)(2,1)S(1)}, bf16[2,64,256]{2,1,0:T(8,128)(2,1)S(1)}, u32[]{:S(2)}, u32[]{:S(2)}) collective-permute-start(bf16[2,64,256]{2,1,0:T(8,128)(2,1)S(1)} %collective-permute-done.12), channel_id=1, source_target_pairs={{0,1},{1,2},{2,3},{3,4},{4,5},{5,6},{6,7},{7,8},{8,9},{9,10},{10,1... | collective-permute-start | bytes 196616 | tf_op jit(solution)/shard_map/ppermute | solution.py:19
  137.6 124.2 %reduce-scatter.3.cloned.1.call-start = ((), (), s32[]{:S(2)}) async-start(), calls=%async_computation.3 | async-start | bytes 2228224 | tf_op jit(solution)/shard_map/reduce_scatter | solution.py:130
  142.0 1.1 copy-start
  150.5 1.1 copy-start
  156.1 3.2 %copy-start.2 = (bf16[256,256]{1,0:T(8,128)(2,1)S(1)}, bf16[256,256]{1,0:T(8,128)(2,1)}, u32[]{:S(2)}) copy-start(bf16[256,256]{1,0:T(8,128)(2,1)} %param.20) | copy-start | bytes 393220
  159.1 125.3 %all-reduce.2.cloned.1.call-start = ((), (), s32[]{:S(2)}) async-start(), calls=%async_computation.5 | async-start | bytes 262144 | tf_op jit(solution)/shard_map/psum | solution.py:131
Sparse Core Ops, SparseCore 0:
  12.9 40.7 all-gather.1
  137.7 58.9 reduce-scatter.4
  201.0 60.7 reduce-scatter.2
  263.9 20.4 all-reduce.1
